TPU v7x, 256 devices: a whole 4x4x8 slice. The times are simulated.
256 devices in a mesh: seq: 16 (over z, y_lo), res: 16 (over x, y_hi, core).
Axes of the slice: x: 4, y: 4 (y_hi: 2, y_lo: 2; y = y_hi * 2 + y_lo), z: 8, core: 2. Of those that a mesh axis runs over, the one named last changes fastest.
Arguments:
- alignment_embedding: bfloat16 [256, 512, 768], P('seq', 'res'), may hold values from -12 to 12
- probe_projector: bfloat16 [768, 768], replicated, may hold values from -0.21875 to 0.21875
- lookup_projector: bfloat16 [768, 768], replicated, may hold values from -0.21875 to 0.21875
- content_projector: bfloat16 [768, 768], replicated, may hold values from -0.21875 to 0.21875
- final_projector: bfloat16 [768, 768], replicated, may hold values from -0.21875 to 0.21875
Outputs:
- mixed: bfloat16 [256, 512, 768], P('seq', 'res')
All inputs are finite; a program needn't handle non-finite values.
Results may differ from a plain program's by a relative error of at most 0.01.
Values may be sent and summed in bfloat16 or wider, within the bound.
A program may use at most 128 MiB of HBM per device.

v0:
```python
import math

import jax
import jax.numpy as jnp
from jax import lax
from jax.experimental import pallas as pl
from jax.experimental.pallas import tpu as pltpu
from jax.sharding import PartitionSpec as P

MESH = pl.DeviceIdType.MESH
BF16, F32 = jnp.bfloat16, jnp.float32

H = 12
E = 64
D = 768
ROWS = 16
COLS = 32
NSEQ = 16
HD = D // 2
NP = HD // 128
SITES = 512

O, Y, L, R, YL, YR, OPP, YOPP = range(8)
PARTS = {b: ((0, 5), (5, 4), (9, 3), (12, 4)) for b in range(8)}
PARTS[YOPP] = ((0, 5), (5, 5), (10, 3), (13, 3))
UNIT = 2 * COLS
NZ = 8
OWNED = HD * UNIT // E // NZ
PIECE = OWNED // 2


def kernel(
    x_hbm,
    wq_hbm,
    wk_hbm,
    wv_hbm,
    wo_hbm,
    out_hbm,
    xs,
    wq,
    wkv,
    wo,
    qp,
    kp,
    vp,
    ls,
    lbuf,
    rz,
    sz,
    ry,
    pall,
    factors,
    pfull,
    parts,
    half,
    full,
    in_sem,
    out_sem,
    tx_sem,
    rx_sem,
    mate_sem,
    ltx_sem,
    lrx_sem,
    ytx_sem,
    yrx_sem,
    ptx_sem,
    prx_sem,
    ftx_sem,
    frx_sem,
    htx_sem,
    hrx_sem,
):
    s, r = lax.axis_index("seq"), lax.axis_index("res")
    z, yl = s // 2, lax.rem(s, 2)
    ix, yh, core = r // 4, lax.rem(r // 2, 2), lax.rem(r, 2)

    def at(dx, dy, dc):
        return (s, lax.rem(ix + dx + 4, 4) * 4 + lax.rem(yh + dy, 2) * 2 + lax.rem(core + dc, 2))

    right, left, across, mate = at(1, 0, 0), at(-1, 0, 0), at(0, 1, 0), at(0, 0, 1)

    def above(d):
        return (lax.rem(z + d, NZ) * 2 + yl, r)

    twin = (z * 2 + 1 - yl, r)

    barrier = pltpu.get_barrier_semaphore()
    for device in (right, left, across, mate, twin, *(above(d) for d in range(1, NZ))):
        pl.semaphore_signal(barrier, inc=1, device_id=device, device_id_type=MESH)

    mine = pl.ds(pl.multiple_of(core * HD, HD), HD)
    others = pl.ds(pl.multiple_of((1 - core) * HD, HD), HD)
    loads = [
        pltpu.make_async_copy(x_hbm, xs.at[O, 0], in_sem.at[0]),
        pltpu.make_async_copy(wq_hbm.at[:, mine], wq, in_sem.at[1]),
        pltpu.make_async_copy(wk_hbm.at[:, mine], wkv.at[:, pl.ds(0, HD)], in_sem.at[2]),
        pltpu.make_async_copy(wv_hbm.at[:, mine], wkv.at[:, pl.ds(HD, HD)], in_sem.at[3]),
        pltpu.make_async_copy(wo_hbm.at[mine, :], wo.at[pl.ds(0, HD)], in_sem.at[4]),
        pltpu.make_async_copy(wo_hbm.at[others, :], wo.at[pl.ds(HD, HD)], in_sem.at[5]),
    ]
    for copy in loads:
        copy.start()
    pl.semaphore_wait(barrier, 5 + NZ - 1)

    def send(block, part, device, landing):
        rows = pl.ds(*PARTS[landing][part])
        pltpu.make_async_remote_copy(
            src_ref=x_hbm.at[rows] if block == O else xs.at[block, 0, rows],
            dst_ref=xs.at[landing, 0, rows],
            send_sem=tx_sem.at[0],
            recv_sem=rx_sem.at[landing, part],
            device_id=device,
            device_id_type=MESH,
        ).start()

    def hand_on(block, part):
        rows = pl.ds(*PARTS[block][part])
        pltpu.make_async_remote_copy(
            src_ref=x_hbm.at[rows] if block == O else xs.at[block, 0, rows],
            dst_ref=xs.at[block, 1, rows],
            send_sem=tx_sem.at[1],
            recv_sem=mate_sem.at[block, part // 2],
            device_id=mate,
            device_id_type=MESH,
        ).start()

    def received(ref, recv_sem):
        return pltpu.make_async_remote_copy(
            src_ref=ref,
            dst_ref=ref,
            send_sem=tx_sem.at[0],
            recv_sem=recv_sem,
            device_id=mate,
            device_id_type=MESH,
        )

    def take(block, *parts):
        for part in parts:
            received(xs.at[block, 0, pl.ds(*PARTS[block][part])], rx_sem.at[block, part]).wait_recv()
            hand_on(block, part)

    def from_mate(block, *halves):
        for side in halves or (0, 1):
            (first, some), (_, more) = PARTS[block][2 * side : 2 * side + 2]
            ref = xs.at[block, 1, pl.ds(first, some + more)]
            received(ref, mate_sem.at[block, side]).wait_recv()

    def project_rows(block, cr, first, rows, pairs):
        x = xs[block, cr, pl.ds(first, rows)].reshape(rows * COLS, D)
        w = wkv[:, pl.ds(pairs[0] * 128, len(pairs) * 128)]
        y = jnp.dot(x, w, preferred_element_type=F32).astype(BF16)
        j = pl.ds(pl.multiple_of((2 * block + cr) * COLS, COLS), COLS)
        for row in range(rows):
            lanes = pl.ds((first + row) * 128, 128)
            for n, pair in enumerate(pairs):
                here = y[row * COLS : (row + 1) * COLS, n * 128 : (n + 1) * 128]
                if pair < NP:
                    kp[pair, j, lanes] = here
                else:
                    vp[pair - NP, j, lanes] = here

    def project_kv(block, pairs=range(2 * NP)):
        def one(cr, _):
            project_rows(block, cr, 0, ROWS, pairs)
            return 0

        lax.fori_loop(0, 2, one, 0)

    early, late = range(0, NP + 1), range(NP + 1, 2 * NP)

    def project_part(block, cr, side):
        (first, some), (_, more) = PARTS[block][2 * side : 2 * side + 2]
        project_rows(block, cr, first, some + more, early)

    def project_q(cr):
        x = xs[O, cr].reshape(ROWS * COLS, D)
        y = jnp.dot(x, wq[...], preferred_element_type=F32).astype(BF16)
        low = lax.broadcasted_iota(jnp.int32, (COLS, 128), 1) < E
        zero = jnp.zeros((COLS, 128), BF16)
        for row in range(ROWS):
            for pair in range(NP):
                q = y[row * COLS : (row + 1) * COLS, pair * 128 : (pair + 1) * 128]
                lanes = pl.ds(row * 128, 128)
                qp[pair, pl.ds(cr * COLS, COLS), lanes] = jnp.where(low, q, zero)
                qp[pair, pl.ds(2 * COLS + cr * COLS, COLS), lanes] = jnp.where(low, zero, q)

    low = lax.broadcasted_iota(jnp.int32, (PIECE, 128), 1) < UNIT

    def logits(unit):
        for pair in range(NP):
            k = kp[pair, pl.ds(unit * UNIT, UNIT), :]
            lbuf[pl.ds(pair * 128, 128), :] = lax.dot_general(
                qp[pair],
                jnp.concatenate([k, k], axis=0),
                (((1,), (1,)), ((), ())),
                preferred_element_type=F32,
            )
        for owner in range(NZ):
            ls[unit, owner] = jnp.where(
                low,
                lbuf[pl.ds(owner * OWNED, PIECE), :],
                lbuf[pl.ds(owner * OWNED + PIECE, PIECE), :],
            )

        def along_z(d, _):
            to = lax.rem(z + d, NZ)
            pltpu.make_async_remote_copy(
                src_ref=ls.at[unit, to],
                dst_ref=rz.at[unit, z],
                send_sem=ltx_sem,
                recv_sem=lrx_sem.at[unit],
                device_id=(to * 2 + yl, r),
                device_id_type=MESH,
            ).start()
            return 0

        lax.fori_loop(1, NZ, along_z, 0)
        rz[unit, z] = ls[unit, z]

    scale = 1.0 / math.sqrt(E * ROWS * NSEQ)

    def group(ref, send_sem, recv_sem):
        return pltpu.make_async_remote_copy(
            src_ref=ref,
            dst_ref=ref,
            send_sem=send_sem,
            recv_sem=recv_sem,
            device_id=mate,
            device_id_type=MESH,
        )

    def fold(unit):
        group(rz.at[unit, pl.ds(0, NZ - 1)], ltx_sem, lrx_sem.at[unit]).wait_recv()
        sz[unit] = jnp.sum(rz[unit], axis=0)
        pltpu.make_async_remote_copy(
            src_ref=sz.at[unit],
            dst_ref=ry.at[unit],
            send_sem=ytx_sem,
            recv_sem=yrx_sem.at[unit],
            device_id=twin,
            device_id_type=MESH,
        ).start()

    def halves(reduce, x, fill):
        first = reduce(jnp.where(low, x, fill), axis=1, keepdims=True)
        second = reduce(jnp.where(low, fill, x), axis=1, keepdims=True)
        return jnp.where(low, first, second)

    def scores_of(unit):
        group(ry.at[unit], ytx_sem, yrx_sem.at[unit]).wait_recv()
        return (sz[unit] + ry[unit]) * scale

    stats = []

    def absorb(*units):
        scores = [scores_of(unit) for unit in units]
        top = scores[0]
        for other in scores[1:]:
            top = jnp.maximum(top, other)
        top = halves(jnp.max, top, -jnp.inf)
        total = jnp.zeros((PIECE, 128), F32)
        for unit, score in zip(units, scores):
            weights = jnp.exp(score - top)
            total = total + weights
            pall[z, unit] = weights.astype(BF16)
        stats.append((top, halves(jnp.sum, total, 0.0)))

    def to_line(ref, send_sem, recv_sem):
        def one(d, _):
            pltpu.make_async_remote_copy(
                src_ref=ref,
                dst_ref=ref,
                send_sem=send_sem,
                recv_sem=recv_sem,
                device_id=above(d),
                device_id_type=MESH,
            ).start()
            return 0

        lax.fori_loop(1, NZ, one, 0)

    def spread(first, count, number):
        to_line(pall.at[z, pl.ds(first, count)], ptx_sem, prx_sem.at[number])

    def shared(first, count, number):
        ref = pall.at[pl.ds(0, NZ - 1), pl.ds(first, count)]
        group(ref, ptx_sem, prx_sem.at[number]).wait_recv()

    lane = lax.broadcasted_iota(jnp.int32, (PIECE, 128), 1)
    row_of = lax.broadcasted_iota(jnp.int32, (PIECE, 128), 0)

    def finish(unit):
        scores = scores_of(unit)
        top = halves(jnp.max, scores, -jnp.inf)
        for earlier, _ in stats:
            top = jnp.maximum(top, earlier)
        weights = jnp.exp(scores - top)
        total = halves(jnp.sum, weights, 0.0)
        scales = [jnp.exp(earlier - top) for earlier, _ in stats]
        for earlier, (_, part) in zip(scales, stats):
            total = total + earlier * part
        pall[z, unit] = (weights / total).astype(BF16)
        spread(unit, 1, 3)
        placed = jnp.zeros((PIECE, 128), F32)
        for number, earlier in enumerate(scales):
            here = lax.rem(lane, UNIT) == row_of + 32 * number
            placed = jnp.where(here, earlier / total, placed)
        factors[z] = jnp.sum(placed, axis=0, keepdims=True)
        to_line(factors.at[z], ftx_sem, frx_sem)

    def unpack(left_unit, right_unit, tile):
        even, odd = (
            pall[:, u].astype(F32).reshape(NZ * PIECE, 128) for u in (left_unit, right_unit)
        )
        wide = lax.broadcasted_iota(jnp.int32, (NZ * PIECE, 128), 1) < UNIT
        first = jnp.where(wide, even, pltpu.roll(odd, UNIT, 1))
        second = jnp.where(wide, pltpu.roll(even, UNIT, 1), odd)
        lanes = pl.ds(tile * 128, 128)
        for n, rows in enumerate((first, second)):
            pfull[:, pl.ds(n * PIECE, PIECE), lanes] = rows.astype(BF16).reshape(NZ, PIECE, 128)

    def factor(number):
        l = lax.broadcasted_iota(jnp.int32, (OWNED, 128), 1)
        i = lax.broadcasted_iota(jnp.int32, (OWNED, 128), 0)
        at_lane = jnp.where(i < PIECE, i, i - PIECE + UNIT) + 32 * number
        row = jnp.broadcast_to(factors[...], (NZ, OWNED, 128))
        return jnp.sum(jnp.where((l == at_lane)[None], row, 0.0), axis=2, keepdims=True)

    first_head = lax.broadcasted_iota(jnp.int32, (2 * COLS, 128), 1) < E

    def by_head(x):
        return jnp.where(first_head, x[: 2 * COLS], x[2 * COLS :])

    def product(pair, tile, first, count):
        probs = pfull[:, :, pl.ds(tile * 128, -(-count // 128) * 128)].reshape(NP * 128, -1)
        probs = probs[pair * 128 : (pair + 1) * 128, :count]
        return jnp.dot(probs, vp[pair, pl.ds(first, count), :], preferred_element_type=F32)

    def attend(number, tile, first, count):
        for pair in range(NP):
            whole = product(pair, tile, first, count)
            for row in range(ROWS):
                cut = slice(row * 128, (row + 1) * 128)
                parts[number, pair, :, cut] = by_head(whole[:, cut])

    for part in (2, 3, 0, 1):
        send(O, part, right, L)
    for part in (3, 2, 1, 0):
        send(O, part, left, R)
    for part in range(4):
        send(O, part, across, Y)
    for part in range(4):
        hand_on(O, part)

    for copy in loads[:4]:
        copy.wait()
    project_q(0)
    from_mate(O)
    project_q(1)
    project_kv(O)
    take(L, 2)
    send(L, 2, right, OPP)
    take(R, 3)
    send(R, 3, left, OPP)
    logits(O)
    take(L, 3)
    take(R, 2)
    for part in (2, 3):
        send(L, part, across, YL)
    take(Y, 0, 1)
    for part in (0, 1):
        send(Y, part, right, YL)
    for part in (1, 0):
        send(Y, part, left, YR)
    take(L, 0)
    send(L, 0, right, OPP)
    take(R, 1)
    send(R, 1, left, OPP)
    take(Y, 2)
    take(L, 1)
    take(R, 0)
    take(Y, 3)
    from_mate(L)
    project_kv(L)
    send(R, 2, across, YR)
    logits(L)
    from_mate(R)
    project_kv(R)
    logits(R)
    take(OPP, 2, 3)
    from_mate(Y)
    project_kv(Y)
    logits(Y)
    take(YL, 0)
    send(YL, 0, right, YOPP)
    take(YR, 1, 2)
    send(YR, 1, left, YOPP)
    take(YL, 2, 3)
    fold(O)
    fold(L)
    send(R, 3, across, YR)
    take(YL, 1)
    fold(R)
    take(YR, 0)
    fold(Y)
    for part in (2, 3):
        send(OPP, part, across, YOPP)
    from_mate(YL)
    project_kv(YL)
    logits(YL)
    take(YR, 3)
    take(OPP, 0, 1)
    absorb(O, Y, L, R)
    spread(O, 2, 0)
    from_mate(YR)
    project_kv(YR)
    logits(YR)
    from_mate(OPP)
    project_kv(OPP)
    logits(OPP)
    take(YOPP, 2, 3)
    project_part(YOPP, 0, 1)
    take(YOPP, 0, 1)
    project_part(YOPP, 0, 0)
    from_mate(YOPP, 1)
    project_part(YOPP, 1, 1)
    from_mate(YOPP, 0)
    project_part(YOPP, 1, 0)
    logits(YOPP)

    spread(L, 2, 1)
    fold(YL)
    fold(YR)
    project_kv(YOPP, late)
    shared(O, 2, 0)
    unpack(O, Y, 0)
    fold(OPP)
    absorb(YL, YR, OPP)
    spread(YL, 3, 2)
    fold(YOPP)
    shared(L, 2, 1)
    unpack(L, R, 1)
    attend(0, 0, O * UNIT, 4 * UNIT)
    finish(YOPP)
    shared(YL, 3, 2)
    unpack(YL, YR, 2)
    unpack(OPP, OPP, 3)
    attend(1, 2, YL * UNIT, 3 * UNIT)
    group(factors.at[pl.ds(0, NZ - 1)], ftx_sem, frx_sem).wait_recv()
    scaling = [factor(number).reshape(NP * 128, 1) for number in range(2)]
    shared(YOPP, 1, 3)
    unpack(YOPP, YOPP, 4)

    handed = []
    for pair in range(NP):
        lanes = pl.ds(pair * 128, 128)
        last = product(pair, 4, YOPP * UNIT, UNIT)
        ranks = [by_head(jnp.broadcast_to(f[pair * 128 : (pair + 1) * 128], (128, 128))) for f in scaling]
        for row in range(ROWS):
            cut = slice(row * 128, (row + 1) * 128)
            picked = by_head(last[:, cut])
            for number, rank in enumerate(ranks):
                picked = picked + rank * parts[number, pair, :, cut]
            picked = picked.astype(BF16)
            full[row, :, lanes] = picked[:COLS]
            half[pair, row] = picked[COLS:]
        copy = pltpu.make_async_remote_copy(
            src_ref=half.at[pair],
            dst_ref=full.at[:, :, pl.ds(HD + pair * 128, 128)],
            send_sem=htx_sem.at[pair],
            recv_sem=hrx_sem.at[pair],
            device_id=mate,
            device_id_type=MESH,
        )
        copy.start()
        handed.append(copy)
    for copy in loads[4:]:
        copy.wait()
    for copy in handed:
        copy.wait_recv()
    stored = []
    for quarter in range(4):
        rows = pl.ds(quarter * 4, 4)
        mixed = jnp.dot(full[rows].reshape(4 * COLS, D), wo[...], preferred_element_type=F32)
        full[rows] = mixed.astype(BF16).reshape(4, COLS, D)
        copy = pltpu.make_async_copy(full.at[rows], out_hbm.at[rows], out_sem.at[quarter])
        copy.start()
        stored.append(copy)

    for count, way in ((7, 0), (8, 1)):
        ref = xs.at[pl.ds(0, count), 0]
        pltpu.make_async_remote_copy(
            src_ref=ref,
            dst_ref=ref,
            send_sem=tx_sem.at[way],
            recv_sem=mate_sem.at[0, 0],
            device_id=mate,
            device_id_type=MESH,
        ).wait_send()
    group(rz.at[:, pl.ds(0, NZ - 1)], ltx_sem, lrx_sem.at[0]).wait_send()
    group(sz, ytx_sem, yrx_sem.at[0]).wait_send()
    group(pall.at[pl.ds(0, NZ - 1)], ptx_sem, prx_sem.at[0]).wait_send()
    group(factors.at[pl.ds(0, NZ - 1)], ftx_sem, frx_sem).wait_send()
    for copy in handed:
        copy.wait_send()
    for copy in stored:
        copy.wait()


def body(alignment_embedding, probe_projector, lookup_projector, content_projector, final_projector):
    hbm = pl.BlockSpec(memory_space=pl.ANY)
    return pl.pallas_call(
        kernel,
        out_shape=jax.ShapeDtypeStruct((ROWS, COLS, D), BF16),
        in_specs=[hbm] * 5,
        out_specs=hbm,
        scratch_shapes=[
            pltpu.VMEM((8, 2, ROWS, COLS, D), BF16),
            pltpu.VMEM((D, HD), BF16),
            pltpu.VMEM((D, D), BF16),
            pltpu.VMEM((D, D), BF16),
            pltpu.VMEM((NP, 4 * COLS, ROWS * 128), BF16),
            pltpu.VMEM((NP, SITES, ROWS * 128), BF16),
            pltpu.VMEM((NP, SITES, ROWS * 128), BF16),
            pltpu.VMEM((8, NZ, PIECE, 128), F32),
            pltpu.VMEM((NP * 128, 128), F32),
            pltpu.VMEM((8, NZ, PIECE, 128), F32),
            pltpu.VMEM((8, PIECE, 128), F32),
            pltpu.VMEM((8, PIECE, 128), F32),
            pltpu.VMEM((NZ, 8, PIECE, 128), BF16),
            pltpu.VMEM((NZ, 1, 128), F32),
            pltpu.VMEM((NZ, OWNED, SITES + 128), BF16),
            pltpu.VMEM((2, NP, 2 * COLS, ROWS * 128), F32),
            pltpu.VMEM((NP, ROWS, COLS, 128), BF16),
            pltpu.VMEM((ROWS, COLS, D), BF16),
            pltpu.SemaphoreType.DMA((6,)),
            pltpu.SemaphoreType.DMA((4,)),
            pltpu.SemaphoreType.DMA((2,)),
            pltpu.SemaphoreType.DMA((8, 4)),
            pltpu.SemaphoreType.DMA((8, 2)),
            pltpu.SemaphoreType.DMA,
            pltpu.SemaphoreType.DMA((8,)),
            pltpu.SemaphoreType.DMA,
            pltpu.SemaphoreType.DMA((8,)),
            pltpu.SemaphoreType.DMA,
            pltpu.SemaphoreType.DMA((4,)),
            pltpu.SemaphoreType.DMA,
            pltpu.SemaphoreType.DMA,
            pltpu.SemaphoreType.DMA((NP,)),
            pltpu.SemaphoreType.DMA((NP,)),
        ],
        compiler_params=pltpu.CompilerParams(
            collective_id=0, has_side_effects=True, vmem_limit_bytes=58 * 2**20
        ),
        name="tied_rows",
    )(
        alignment_embedding,
        probe_projector,
        lookup_projector,
        content_projector,
        final_projector,
    )


def solution(mesh):
    placed = (P("seq", "res", None), P(), P(), P(), P())
    return jax.shard_map(
        body, mesh=mesh, in_specs=placed, out_specs=P("seq", "res", None), check_vma=False
    )
```

profile of v0, /device:TPU:1, one launch (start us, length us, event | category | flops | bytes accessed | tf_op | source)
XLA Modules:
  0.0 77.4 jit_solution(3780999701193559272)
XLA Ops:
  0.0 75.3 %tied_rows.1 = bf16[16,32,768]{2,1,0:T(8,128)(2,1)} custom-call(bf16[16,32,768]{2,1,0:T(8,128)(2,1)} %x_hbm.1, bf16[768,768]{1,0:T(8,128)(2,1)} %wq_hbm.1, bf16[768,768]{1,0:T(8,128)(2,1)} %wk_hbm.1, bf16[768,768]{1,0:T(8,128)(2,1)} %wv_hbm.1, bf16[768,768]{1,0:T(8,128)(2,1)} %wo_hbm.1), custom_call_target="tpu_custom_call" | custom-call | tf_op jit(solution)/shard_map/tied_rows/pallas_call | solution.py:512
  75.3 2.1 %copy.7 = bf16[16,32,768]{2,1,0:T(8,128)(2,1)} copy(bf16[16,32,768]{2,1,0:T(8,128)(2,1)} %tied_rows.1) | data formatting | bytes 1572864
where the time goes:
time: 77.5 us; the launch traced here: 77.4 us
  Pallas kernels  75.3 us (97%)
  local copies, waits for them, and re-layouts  2.06 us (3%)
    pallas_call x1, Pallas kernels, body(): pl.pallas_call(kernel, out_shape=jax.ShapeDtypeStruct((ROWS, COLS, D), BF...  75.3 us
    unnamed x1, local copies, waits for them, and re-layouts  2.06 us

commit v1 on v0

--- a/solution.py
+++ b/solution.py
@@ -35,7 +35,7 @@
     wk_hbm,
     wv_hbm,
     wo_hbm,
-    out_hbm,
+    out_ref,
     xs,
     wq,
     wkv,
@@ -55,7 +55,6 @@
     half,
     full,
     in_sem,
-    out_sem,
     tx_sem,
     rx_sem,
     mate_sem,
@@ -478,14 +477,10 @@
         copy.wait()
     for copy in handed:
         copy.wait_recv()
-    stored = []
     for quarter in range(4):
         rows = pl.ds(quarter * 4, 4)
         mixed = jnp.dot(full[rows].reshape(4 * COLS, D), wo[...], preferred_element_type=F32)
-        full[rows] = mixed.astype(BF16).reshape(4, COLS, D)
-        copy = pltpu.make_async_copy(full.at[rows], out_hbm.at[rows], out_sem.at[quarter])
-        copy.start()
-        stored.append(copy)
+        out_ref[rows] = mixed.astype(BF16).reshape(4, COLS, D)
 
     for count, way in ((7, 0), (8, 1)):
         ref = xs.at[pl.ds(0, count), 0]
@@ -503,8 +498,6 @@
     group(factors.at[pl.ds(0, NZ - 1)], ftx_sem, frx_sem).wait_send()
     for copy in handed:
         copy.wait_send()
-    for copy in stored:
-        copy.wait()
 
 
 def body(alignment_embedding, probe_projector, lookup_projector, content_projector, final_projector):
@@ -513,7 +506,7 @@
         kernel,
         out_shape=jax.ShapeDtypeStruct((ROWS, COLS, D), BF16),
         in_specs=[hbm] * 5,
-        out_specs=hbm,
+        out_specs=pl.BlockSpec(memory_space=pltpu.VMEM),
         scratch_shapes=[
             pltpu.VMEM((8, 2, ROWS, COLS, D), BF16),
             pltpu.VMEM((D, HD), BF16),
@@ -534,7 +527,6 @@
             pltpu.VMEM((NP, ROWS, COLS, 128), BF16),
             pltpu.VMEM((ROWS, COLS, D), BF16),
             pltpu.SemaphoreType.DMA((6,)),
-            pltpu.SemaphoreType.DMA((4,)),
             pltpu.SemaphoreType.DMA((2,)),
             pltpu.SemaphoreType.DMA((8, 4)),
             pltpu.SemaphoreType.DMA((8, 2)),
@@ -550,7 +542,7 @@
             pltpu.SemaphoreType.DMA((NP,)),
         ],
         compiler_params=pltpu.CompilerParams(
-            collective_id=0, has_side_effects=True, vmem_limit_bytes=58 * 2**20
+            collective_id=0, has_side_effects=True, vmem_limit_bytes=53 * 2**20
         ),
         name="tied_rows",
     )(

time: 77.5 us -> 75.6 us (0.975)
  local copies, waits for them, and re-layouts: 2.06 us -> 0.88 us
    unnamed x1, local copies, waits for them, and re-layouts: 2.06 us -> 0.88 us
where the time goes in v1:
time: 75.6 us; the launch traced here: 75.5 us
  Pallas kernels  74.6 us (99%)
  local copies, waits for them, and re-layouts  0.88 us (1%)
    pallas_call x1, Pallas kernels, body(): pl.pallas_call(kernel, out_shape=jax.ShapeDtypeStruct((ROWS, COLS, D), BF...  74.6 us

profile of v1, /device:TPU:1, one launch (start us, length us, event | category | flops | bytes accessed | tf_op | source)
XLA Modules:
  0.0 75.5 jit_solution(13700447553130138477)
XLA Ops:
  0.0 74.6 %tied_rows.1 = bf16[16,32,768]{2,1,0:T(8,128)(2,1)S(1)} custom-call(bf16[16,32,768]{2,1,0:T(8,128)(2,1)} %x_hbm.1, bf16[768,768]{1,0:T(8,128)(2,1)} %wq_hbm.1, bf16[768,768]{1,0:T(8,128)(2,1)} %wk_hbm.1, bf16[768,768]{1,0:T(8,128)(2,1)} %wv_hbm.1, bf16[768,768]{1,0:T(8,128)(2,1)} %wo_hbm.1), custom_call_target="tpu_custom_call" | custom-call | tf_op jit(solution)/shard_map/tied_rows/pallas_call | solution.py:505
  74.6 0.9 %copy.7 = bf16[16,32,768]{2,1,0:T(8,128)(2,1)} copy(bf16[16,32,768]{2,1,0:T(8,128)(2,1)S(1)} %tied_rows.1) | data formatting | bytes 1572864

commit v2 on v1

--- a/solution.py
+++ b/solution.py
@@ -78,6 +78,9 @@
 
     right, left, across, mate = at(1, 0, 0), at(-1, 0, 0), at(0, 1, 0), at(0, 0, 1)
 
+    def far_first(k):
+        return 4 + (k + 1) // 2 * (1 - 2 * lax.rem(k, 2))
+
     def above(d):
         return (lax.rem(z + d, NZ) * 2 + yl, r)
 
@@ -201,8 +204,8 @@
                 lbuf[pl.ds(owner * OWNED + PIECE, PIECE), :],
             )
 
-        def along_z(d, _):
-            to = lax.rem(z + d, NZ)
+        def along_z(k, _):
+            to = lax.rem(z + far_first(k), NZ)
             pltpu.make_async_remote_copy(
                 src_ref=ls.at[unit, to],
                 dst_ref=rz.at[unit, z],
@@ -213,7 +216,7 @@
             ).start()
             return 0
 
-        lax.fori_loop(1, NZ, along_z, 0)
+        lax.fori_loop(0, NZ - 1, along_z, 0)
         rz[unit, z] = ls[unit, z]
 
     scale = 1.0 / math.sqrt(E * ROWS * NSEQ)
@@ -265,18 +268,18 @@
         stats.append((top, halves(jnp.sum, total, 0.0)))
 
     def to_line(ref, send_sem, recv_sem):
-        def one(d, _):
+        def one(k, _):
             pltpu.make_async_remote_copy(
                 src_ref=ref,
                 dst_ref=ref,
                 send_sem=send_sem,
                 recv_sem=recv_sem,
-                device_id=above(d),
+                device_id=above(far_first(k)),
                 device_id_type=MESH,
             ).start()
             return 0
 
-        lax.fori_loop(1, NZ, one, 0)
+        lax.fori_loop(0, NZ - 1, one, 0)
 
     def spread(first, count, number):
         to_line(pall.at[z, pl.ds(first, count)], ptx_sem, prx_sem.at[number])
@@ -418,8 +421,8 @@
     project_kv(OPP)
     logits(OPP)
     take(YOPP, 2, 3)
+    take(YOPP, 0, 1)
     project_part(YOPP, 0, 1)
-    take(YOPP, 0, 1)
     project_part(YOPP, 0, 0)
     from_mate(YOPP, 1)
     project_part(YOPP, 1, 1)
@@ -477,10 +480,8 @@
         copy.wait()
     for copy in handed:
         copy.wait_recv()
-    for quarter in range(4):
-        rows = pl.ds(quarter * 4, 4)
-        mixed = jnp.dot(full[rows].reshape(4 * COLS, D), wo[...], preferred_element_type=F32)
-        out_ref[rows] = mixed.astype(BF16).reshape(4, COLS, D)
+    mixed = jnp.dot(full[...].reshape(ROWS * COLS, D), wo[...], preferred_element_type=F32)
+    out_ref[...] = mixed.astype(BF16).reshape(ROWS, COLS, D)
 
     for count, way in ((7, 0), (8, 1)):
         ref = xs.at[pl.ds(0, count), 0]

time: 75.6 us -> 75 us (level)
  no operation moved by 1% of the time
where the time goes in v2:
time: 75 us
  Pallas kernels  74.1 us (99%)
  local copies, waits for them, and re-layouts  0.88 us (1%)
    pallas_call x1, Pallas kernels, body(): pl.pallas_call(kernel, out_shape=jax.ShapeDtypeStruct((ROWS, COLS, D), BF...  74.1 us

profile of v2, /device:TPU:1, one launch (start us, length us, event | category | flops | bytes accessed | tf_op | source)
XLA Modules:
  0.0 75.0 jit_solution(571062282315310529)
XLA Ops:
  0.0 74.1 %tied_rows.1 = bf16[16,32,768]{2,1,0:T(8,128)(2,1)S(1)} custom-call(bf16[16,32,768]{2,1,0:T(8,128)(2,1)} %x_hbm.1, bf16[768,768]{1,0:T(8,128)(2,1)} %wq_hbm.1, bf16[768,768]{1,0:T(8,128)(2,1)} %wk_hbm.1, bf16[768,768]{1,0:T(8,128)(2,1)} %wv_hbm.1, bf16[768,768]{1,0:T(8,128)(2,1)} %wo_hbm.1), custom_call_target="tpu_custom_call" | custom-call | tf_op jit(solution)/shard_map/tied_rows/pallas_call | solution.py:506
  74.1 0.9 %copy.7 = bf16[16,32,768]{2,1,0:T(8,128)(2,1)} copy(bf16[16,32,768]{2,1,0:T(8,128)(2,1)S(1)} %tied_rows.1) | data formatting | bytes 1572864

commit v3 on v2

--- a/solution.py
+++ b/solution.py
@@ -430,20 +430,20 @@
     project_part(YOPP, 1, 0)
     logits(YOPP)
 
-    spread(L, 2, 1)
     fold(YL)
     fold(YR)
     project_kv(YOPP, late)
     shared(O, 2, 0)
     unpack(O, Y, 0)
     fold(OPP)
+    spread(L, 2, 1)
     absorb(YL, YR, OPP)
     spread(YL, 3, 2)
     fold(YOPP)
+    finish(YOPP)
     shared(L, 2, 1)
     unpack(L, R, 1)
     attend(0, 0, O * UNIT, 4 * UNIT)
-    finish(YOPP)
     shared(YL, 3, 2)
     unpack(YL, YR, 2)
     unpack(OPP, OPP, 3)

time: 75 us -> 74.7 us (level)
  no operation moved by 1% of the time
where the time goes in v3:
time: 74.7 us; the launch traced here: 74.6 us
  Pallas kernels  73.7 us (99%)
  local copies, waits for them, and re-layouts  0.88 us (1%)
    pallas_call x1, Pallas kernels, body(): pl.pallas_call(kernel, out_shape=jax.ShapeDtypeStruct((ROWS, COLS, D), BF...  73.7 us

profile of v3, /device:TPU:1, one launch (start us, length us, event | category | flops | bytes accessed | tf_op | source)
XLA Modules:
  0.0 74.6 jit_solution(12160334212657705238)
XLA Ops:
  0.0 73.7 %tied_rows.1 = bf16[16,32,768]{2,1,0:T(8,128)(2,1)S(1)} custom-call(bf16[16,32,768]{2,1,0:T(8,128)(2,1)} %x_hbm.1, bf16[768,768]{1,0:T(8,128)(2,1)} %wq_hbm.1, bf16[768,768]{1,0:T(8,128)(2,1)} %wk_hbm.1, bf16[768,768]{1,0:T(8,128)(2,1)} %wv_hbm.1, bf16[768,768]{1,0:T(8,128)(2,1)} %wo_hbm.1), custom_call_target="tpu_custom_call" | custom-call | tf_op jit(solution)/shard_map/tied_rows/pallas_call | solution.py:506
  73.7 0.9 %copy.7 = bf16[16,32,768]{2,1,0:T(8,128)(2,1)} copy(bf16[16,32,768]{2,1,0:T(8,128)(2,1)S(1)} %tied_rows.1) | data formatting | bytes 1572864

commit v4 on v3

--- a/solution.py
+++ b/solution.py
@@ -188,15 +188,21 @@
 
     low = lax.broadcasted_iota(jnp.int32, (PIECE, 128), 1) < UNIT
 
-    def logits(unit):
+    def multiply(unit, first, rows, more=False):
+        lanes = pl.ds(first * 128, rows * 128)
         for pair in range(NP):
-            k = kp[pair, pl.ds(unit * UNIT, UNIT), :]
-            lbuf[pl.ds(pair * 128, 128), :] = lax.dot_general(
-                qp[pair],
+            k = kp[pair, pl.ds(unit * UNIT, UNIT), lanes]
+            part = lax.dot_general(
+                qp[pair, :, lanes],
                 jnp.concatenate([k, k], axis=0),
                 (((1,), (1,)), ((), ())),
                 preferred_element_type=F32,
             )
+            here = pl.ds(pair * 128, 128)
+            lbuf[here, :] = lbuf[here, :] + part if more else part
+
+    def logits(unit, done=ROWS):
+        multiply(unit, 0, done, done < ROWS)
         for owner in range(NZ):
             ls[unit, owner] = jnp.where(
                 low,
@@ -426,9 +432,11 @@
     project_part(YOPP, 0, 0)
     from_mate(YOPP, 1)
     project_part(YOPP, 1, 1)
+    split = PARTS[YOPP][2][0]
+    multiply(YOPP, split, ROWS - split)
     from_mate(YOPP, 0)
     project_part(YOPP, 1, 0)
-    logits(YOPP)
+    logits(YOPP, split)
 
     fold(YL)
     fold(YR)
@@ -448,10 +456,10 @@
     unpack(YL, YR, 2)
     unpack(OPP, OPP, 3)
     attend(1, 2, YL * UNIT, 3 * UNIT)
+    shared(YOPP, 1, 3)
+    unpack(YOPP, YOPP, 4)
     group(factors.at[pl.ds(0, NZ - 1)], ftx_sem, frx_sem).wait_recv()
     scaling = [factor(number).reshape(NP * 128, 1) for number in range(2)]
-    shared(YOPP, 1, 3)
-    unpack(YOPP, YOPP, 4)
 
     handed = []
     for pair in range(NP):

time: 74.7 us -> 74.3 us (level)
  no operation moved by 1% of the time
where the time goes in v4:
time: 74.3 us; the launch traced here: 74.2 us
  Pallas kernels  73.3 us (99%)
  local copies, waits for them, and re-layouts  0.88 us (1%)
    pallas_call x1, Pallas kernels, body(): pl.pallas_call(kernel, out_shape=jax.ShapeDtypeStruct((ROWS, COLS, D), BF...  73.3 us

profile of v4, /device:TPU:1, one launch (start us, length us, event | category | flops | bytes accessed | tf_op | source)
XLA Modules:
  0.0 74.2 jit_solution(13609907282672746904)
XLA Ops:
  0.0 73.3 %tied_rows.1 = bf16[16,32,768]{2,1,0:T(8,128)(2,1)S(1)} custom-call(bf16[16,32,768]{2,1,0:T(8,128)(2,1)} %x_hbm.1, bf16[768,768]{1,0:T(8,128)(2,1)} %wq_hbm.1, bf16[768,768]{1,0:T(8,128)(2,1)} %wk_hbm.1, bf16[768,768]{1,0:T(8,128)(2,1)} %wv_hbm.1, bf16[768,768]{1,0:T(8,128)(2,1)} %wo_hbm.1), custom_call_target="tpu_custom_call" | custom-call | tf_op jit(solution)/shard_map/tied_rows/pallas_call | solution.py:514
  73.3 0.9 %copy.7 = bf16[16,32,768]{2,1,0:T(8,128)(2,1)} copy(bf16[16,32,768]{2,1,0:T(8,128)(2,1)S(1)} %tied_rows.1) | data formatting | bytes 1572864
